TPU v7x, 32 devices: a whole 2x2x4 slice. The times are simulated.
32 devices in a mesh: row: 4 (over x, core), col: 8 (over z, y).
Axes of the slice: x: 2, y: 2, z: 4, core: 2. Of those that a mesh axis runs over, the one named last changes fastest.
Arguments:
- vectors: float32 [512, 4096], P('row', 'col'), may hold values from -6 to 6
- factors: float32 [8, 4, 512, 512], P('col', None, 'row'), may hold values from -1 to 1, as said below
- offsets: int32 [8], replicated, may hold values from 0 to 1
Outputs:
- updated: float32 [512, 4096], P('row', 'col')
Inputs may be any that keep to these rules, and one draw needn't show every extreme that they name: Each factors[c, k] is an orthogonal matrix.
All inputs are finite; a program needn't handle non-finite values.
Results may differ from a plain program's by a relative error of at most 0.00014.
Values sent between devices are 32-bit elements; how exact they have to be, the bound alone decides.
No kernel may reach another device: no remote copies, remote signals or barrier semaphores. Data moves between devices by JAX's collectives and lax.ppermute only.
A program may use at most 64 MiB of HBM per device.

v0:
```python
import functools

import jax
import jax.numpy as jnp
from jax import lax
from jax.experimental import pallas as pl
from jax.experimental.pallas import tpu as pltpu
from jax.sharding import PartitionSpec as P


FACTORS = 4
TICKS = 3


def split_halves(value):
    high = value.astype(jnp.bfloat16)
    low = (value - high.astype(jnp.float32)).astype(jnp.bfloat16)
    return high, low


def product(former, high_ref, low_ref):
    rows = former.shape[0]
    high, low = split_halves(former)
    both = jnp.concatenate([high, low], 0)
    first = jnp.dot(both, high_ref[...], preferred_element_type=jnp.float32)
    second = jnp.dot(high, low_ref[...], preferred_element_type=jnp.float32)
    return first[:rows] + (first[rows:] + second)


def place(groups, offsets_ref):
    column = lax.axis_index("col")
    offset = offsets_ref[column]
    last = 2 * groups - 2 - 2 * column - offset
    return column, lax.rem(column, TICKS), offset, last


def convert(pieces, index, high_ref, low_ref):
    height = pieces[0].shape[1]
    row = lax.axis_index("row")
    for mask, piece in enumerate(pieces):
        high, low = split_halves(piece[index[mask]])
        start = pl.multiple_of((row ^ mask) * height, height)
        high_ref[pl.ds(start, height), :] = high
        low_ref[pl.ds(start, height), :] = low


def strips(first, count, stride):
    return (slice(None), pl.ds(pl.multiple_of(first * stride, stride), count * stride))


def early_kernel(groups, ring, numbers, stride, *refs):
    half = ring // 2
    refs = list(refs)
    offsets_ref = refs.pop(0)
    shift = numbers[0]
    blocks = [refs.pop(0) for _ in range(3 if shift == 0 else 1)]
    pieces = [refs.pop(0) for _ in range(ring)]
    results = [refs.pop(0) for _ in range(3 if shift == 0 else 2)]
    *kept, buf = refs
    _, tick, offset, last = place(groups, offsets_ref)
    active = tick == 0

    @pl.when(active)
    def _():
        width = blocks[0].shape[1]
        for i, block in enumerate(blocks):
            buf[:, i * width : (i + 1) * width] = block[...]

    for i, number in enumerate(numbers):
        index = [number] * half + [i] * half
        if shift == 0:
            convert(pieces, index, kept[2 * i], kept[2 * i + 1])

        @pl.when(active & (number <= last))
        def _():
            if shift != 0:
                convert(pieces, index, kept[2 * i], kept[2 * i + 1])
            begin = 0 if shift == 3 else offset + number - shift
            here = strips(begin, 2, stride)
            buf[here] = product(buf[here], kept[2 * i], kept[2 * i + 1])

    @pl.when(active)
    def _():
        if shift == 0:
            results[0][...] = buf[:, : 2 * stride]
            results[1][...] = buf[:, 2 * stride :]
            results[2][...] = buf[strips(5 - 3 * offset, 1, stride)]
        elif shift == 2:
            results[0][...] = buf[strips(offset, 1, stride)]
            results[1][...] = buf[strips(1 + offset, 2, stride)]
        else:
            upper = buf.shape[0] // 2
            results[0][...] = buf[:upper]
            results[1][...] = buf[upper:]


def ready_kernel(ring, numbers, *refs):
    tick = lax.rem(lax.axis_index("col"), TICKS)
    half = ring // 2
    kept = refs[len(numbers) * ring :]

    @pl.when(tick == TICKS - 1)
    def _():
        for i, (near, away) in enumerate(numbers):
            pieces = refs[i * ring : (i + 1) * ring]
            convert(pieces, [near] * half + [away] * half, *kept[2 * i : 2 * i + 2])


def middle_kernel(groups, part, stride, *refs):
    offsets_ref, ahead, outer, final = refs[:4]
    weights = refs[4 : 4 + FACTORS]
    own, onward, buf = refs[4 + FACTORS :]
    column, tick, offset, last = place(groups, offsets_ref)
    before = offsets_ref[jnp.maximum(column - 1, 0)]

    height = buf.shape[0]

    @pl.when(tick == 1)
    def _():
        these = slice(part * height, (part + 1) * height)
        buf[strips(3 - 3 * before, 1, stride)] = ahead[these]
        buf[strips(before, 1, stride)] = outer[these]
        buf[strips(1 + before, 2, stride)] = final[...]
        for number in range(FACTORS // 2):

            @pl.when(number <= last)
            def _():
                here = strips(offset + number, 2, stride)
                buf[here] = product(buf[here], weights[2 * number], weights[2 * number + 1])

        own[...] = buf[:, : 2 * stride]
        onward[...] = buf[:, 2 * stride :]


def last_kernel(groups, part, turns, stride, *refs):
    count, half = len(turns), FACTORS // 2
    offsets_ref, first, second = refs[:3]
    weights = refs[3 : 3 + 2 * count]
    *results, buf = refs[3 + 2 * count :]
    column, tick, offset, last = place(groups, offsets_ref)
    before = offsets_ref[jnp.maximum(column - 1, 0)]

    height = buf.shape[0]

    @pl.when(tick == TICKS - 1)
    def _():
        buf[:, : 2 * stride] = first[...]
        if second.shape[0] == height:
            buf[:, 2 * stride :] = second[...]
        else:
            buf[:, 2 * stride :] = second[part * height : (part + 1) * height]
        for i, turn in enumerate(turns):
            if turn < half:
                start = before + turn
                valid = turn + half <= last + 2 + offset - before
            else:
                start = offset + turn - half - (half if turns[0] else 0)
                valid = turn - half <= last

            @pl.when(valid)
            def _():
                here = strips(start, 2, stride)
                buf[here] = product(buf[here], weights[2 * i], weights[2 * i + 1])

        results[0][...] = buf[:, : 2 * stride]
        results[1][...] = buf[:, 2 * stride :]


def pick_kernel(own0, *refs):
    *sources, out = refs
    column = lax.axis_index("col")
    tick = lax.rem(column, TICKS)
    height = out.shape[0] // 2

    @pl.when((tick == 0) & (column < TICKS))
    def _():
        out[...] = own0[...]

    for i, chosen in enumerate(
        (
            (tick == 1) & (column < TICKS),
            tick == 2,
            (tick == 0) & (column >= TICKS),
            (tick == 1) & (column >= TICKS),
        )
    ):

        @pl.when(chosen)
        def _():
            out[:height] = sources[2 * i][...]
            out[height:] = sources[2 * i + 1][...]


def on_device(groups, ring, vectors, factors, offsets):
    rows, width = vectors.shape
    stride = width // 2
    height = factors.shape[2]
    order = ring * height
    f32, bf16 = jnp.float32, jnp.bfloat16
    on_chip = pl.BlockSpec(memory_space=pltpu.VMEM)
    scalars = pl.BlockSpec(memory_space=pltpu.SMEM)
    bits = [1 << i for i in range(ring.bit_length() - 1)]
    top = bits.pop()

    def along(array, distance, tick, back=True):
        swaps = {
            i: i + distance
            for i in range(groups)
            if i % TICKS == tick and 0 <= i + distance < groups
        }
        moves = {i: i for i in range(groups)}
        for source, target in swaps.items():
            moves |= {source: target, target: source}
        if not back:
            for target in swaps.values():
                del moves[target]
        pairs = [
            (row * groups + i, (row ^ 1 if i == target else row) * groups + target)
            for row in range(ring)
            for i, target in moves.items()
        ]
        return lax.ppermute(array, ("row", "col"), pairs)

    def across(array, ticks):
        pairs = [
            (row * groups + i, (row ^ (top if i % TICKS in ticks else 1)) * groups + i)
            for row in range(ring)
            for i in range(groups)
        ]
        return lax.ppermute(array, ("row", "col"), pairs)

    def spread(pieces):
        for bit in bits[::-1]:
            for mask in list(pieces):
                pieces[mask ^ bit] = lax.ppermute(
                    pieces[mask], "row", [(i, i ^ bit) for i in range(ring)]
                )
        return [pieces[mask] for mask in sorted(pieces)]

    def call(kernel, outs, scratch, *operands):
        return pl.pallas_call(
            kernel,
            out_shape=outs,
            in_specs=[scalars if op.dtype == jnp.int32 else on_chip for op in operands],
            out_specs=[on_chip] * len(outs),
            scratch_shapes=scratch,
            compiler_params=pltpu.CompilerParams(vmem_limit_bytes=24 << 20),
        )(*operands)

    def block(columns=width, dtype=f32, high=rows):
        return jax.ShapeDtypeStruct((high, columns), dtype)

    def pair(count):
        return [block(order, bf16, order)] * (2 * count)

    half = FACTORS // 2
    whole = factors[0]
    own = spread({0: whole})
    away = {
        0: across(whole[:half], (0, 1, 2)),
        2: across(whole[2:3], (0, 2)),
        3: across(whole[3:], (0,)),
    }
    gathered = {number: own + spread({top: cut}) for number, cut in away.items()}
    handed = along(whole[half:], 1, 1, False)
    crossed = across(handed, (2,))
    handed = spread({0: handed}) + spread({top: crossed})
    mine = own + spread({top: across(whole[3:], (2,))})

    beside = along(vectors, -1, 1)
    distant = along(vectors, -2, 2)

    def early(numbers, blocks, outs):
        span = sum(b.shape[1] for b in blocks)
        return call(
            functools.partial(early_kernel, groups, ring, numbers, stride),
            outs,
            ([] if blocks[1:] else [pltpu.VMEM((order, order), bf16)] * 2)
            + [pltpu.VMEM((rows, span), f32)],
            offsets,
            *blocks,
            *gathered[numbers[0]],
        )

    own0, rest, ahead, *first_pairs = early(
        (0, 1), [vectors, beside, distant], [block(), block(2 * width), block(stride), *pair(2)]
    )
    ahead = along(ahead, 1, 0)
    third = along(own0, -1, 0, False)
    outer, passing = early((2,), [rest], [block(stride), block()])
    outer = along(outer, 1, 0)
    final = early((3,), [passing], [block(high=rows // 2)] * 2)
    final = [along(part, 1, 0) for part in final]

    def ready(numbers, *pieces):
        return call(functools.partial(ready_kernel, ring, numbers), pair(len(numbers)), [], *pieces)

    handed_pairs = ready(((0, 0), (1, 1)), *handed, *handed)
    last_pairs = ready(((2, 0), (3, 0)), *gathered[2], *mine)
    low = block(high=rows // 2)
    buf = pltpu.VMEM((rows // 2, 2 * width), f32)
    own1, onward, fourth, own2, near, far = [], [], [], [], [], []
    for i in range(2):
        kept, sent = call(
            functools.partial(middle_kernel, groups, i, stride),
            [low] * 2,
            [buf],
            offsets,
            ahead,
            outer,
            final[i],
            *first_pairs,
        )
        own1.append(kept)
        onward.append(along(sent, 1, 1))
        fourth.append(along(kept, -2, 1))
    for i in range(2):
        kept, sent = call(
            functools.partial(last_kernel, groups, i, (0, 1, 2, 3), stride),
            [low] * 2,
            [buf],
            offsets,
            onward[i],
            third,
            *handed_pairs,
            *first_pairs,
        )
        own2.append(kept)
        next_block, after = call(
            functools.partial(last_kernel, groups, i, (4, 5), stride),
            [low] * 2,
            [buf],
            offsets,
            sent,
            fourth[i],
            *last_pairs,
        )
        near.append(along(next_block, 1, 2))
        far.append(along(after, 2, 2))
    (out,) = call(pick_kernel, [block()], [], own0, *own1, *own2, *near, *far)
    return out


def solution(mesh):
    placed = (P("row", "col"), P("col", None, "row", None), P())
    ring = mesh.shape["row"]

    def body(*blocks):
        return on_device(mesh.shape["col"], ring, *blocks)

    return jax.shard_map(
        body, mesh=mesh, in_specs=placed, out_specs=P("row", "col"), check_vma=False
    )
```

profile of v0, /device:TPU:28, one launch (start us, length us, event | category | flops | bytes accessed | tf_op | source)
XLA Modules:
  0.0 76.3 jit_solution(15329105748439606244)
XLA Ops:
  0.0 1.4 %slice_bitcast_fusion = (f32[2,128,512]{2,1,0:T(8,128)S(1)}, f32[2,128,512]{2,1,0:T(8,128)S(1)}) fusion(f32[1,4,128,512]{3,2,1,0:T(8,128)} %param.4), kind=kLoop, calls=%fused_computation | loop fusion | bytes 2097152 | tf_op jit(solution)/shard_map/slice | solution.py:265
  1.4 1.6 %collective-permute-start.3 = (f32[2,128,512]{2,1,0:T(8,128)S(1)}, f32[2,128,512]{2,1,0:T(8,128)S(1)}, u32[]{:S(2)}, u32[]{:S(2)}) collective-permute-start(f32[2,128,512]{2,1,0:T(8,128)S(1)} %get-tuple-element.68), channel_id=1, source_target_pairs={{0,16},{1,17},{2,18},{3,19},{4,20},{5,21},{6,22},{7,23},{8,24},{9,... | collective-permute-start | bytes 1572872 | tf_op jit(solution)/shard_map/ppermute | solution.py:230
  2.9 1.9 %collective-permute-start.15 = (f32[2,128,512]{2,1,0:T(8,128)S(1)}, f32[2,128,512]{2,1,0:T(8,128)S(1)}, u32[]{:S(2)}, u32[]{:S(2)}) collective-permute-start(f32[2,128,512]{2,1,0:T(8,128)S(1)} %get-tuple-element.67), channel_id=1, source_target_pairs={{0,8},{1,2},{3,11},{4,5},{6,14},{7,15},{8,0},{9,10},{11,3},{12,13}... | collective-permute-start | bytes 1572872 | tf_op jit(solution)/shard_map/ppermute | solution.py:222
  5.9 9.2 %collective-permute-done.3.refs_6_ = f32[2,128,512]{2,1,0:T(8,128)S(1)} collective-permute-done((f32[2,128,512]{2,1,0:T(8,128)S(1)}, f32[2,128,512]{2,1,0:T(8,128)S(1)}, u32[]{:S(2)}, u32[]{:S(2)}) %collective-permute-start.3) | collective-permute-done | bytes 524320 | tf_op jit(solution)/shard_map/ppermute | solution.py:230
  16.3 1.9 %collective-permute-done.6.refs_4_.refs_2_ = f32[1,128,512]{2,1,0:T(8,128)S(1)} collective-permute-done((f32[1,128,512]{2,1,0:T(8,128)S(1)}, f32[1,128,512]{2,1,0:T(8,128)S(1)}, u32[]{:S(2)}, u32[]{:S(2)}) %collective-permute-start.6) | collective-permute-done | bytes 262176 | tf_op jit(solution)/shard_map/ppermute | solution.py:230
  19.6 0.9 %shard_map.37 = (f32[128,512]{1,0:T(8,128)S(1)}, f32[128,1024]{1,0:T(8,128)S(1)}, f32[128,256]{1,0:T(8,128)S(1)}, bf16[512,512]{1,0:T(8,128)(2,1)S(1)}, bf16[512...) custom-call(s32[8]{0:T(128)S(1)} %copy-done.2, f32[128,512]{1,0:T(8,128)S(1)} %copy-done.1, ...), custom_call_target="tpu_custom_call" | custom-call | tf_op jit(solution)/shard_map/pallas_call | solution.py:241
  20.5 12.5 %collective-permute-start.5 = (f32[128,256]{1,0:T(8,128)S(1)}, f32[128,256]{1,0:T(8,128)S(1)}, u32[]{:S(2)}, u32[]{:S(2)}) collective-permute-start(f32[128,256]{1,0:T(8,128)S(1)} %get-tuple-element.37), channel_id=1, source_target_pairs={{0,1},{1,0},{2,10},{3,4},{4,3},{5,13},{6,7},{7,6},{8,9},{9,8},{10,... | collective-permute-start | bytes 393224 | tf_op jit(solution)/shard_map/ppermute | solution.py:222
  33.0 0.6 shard_map.38
  33.8 0.6 shard_map.39
  34.4 2.4 %collective-permute-done.5.refs_1_ = f32[128,256]{1,0:T(8,128)S(1)} collective-permute-done((f32[128,256]{1,0:T(8,128)S(1)}, f32[128,256]{1,0:T(8,128)S(1)}, u32[]{:S(2)}, u32[]{:S(2)}) %collective-permute-start.5) | collective-permute-done | bytes 131104 | tf_op jit(solution)/shard_map/ppermute | solution.py:222
  36.8 2.5 %collective-permute-start.11 = (f32[64,512]{1,0:T(8,128)S(1)}, f32[64,512]{1,0:T(8,128)S(1)}, u32[]{:S(2)}, u32[]{:S(2)}) collective-permute-start(f32[64,512]{1,0:T(8,128)S(1)} %get-tuple-element.41), channel_id=1, source_target_pairs={{0,1},{1,0},{2,10},{3,4},{4,3},{5,13},{6,7},{7,6},{8,9},{9,8},{10,... | collective-permute-start | bytes 393224 | tf_op jit(solution)/shard_map/ppermute | solution.py:222
  39.3 0.7 collective-permute-done.8.refs_2_
  40.0 1.9 %collective-permute-start.14 = (f32[128,512]{1,0:T(8,128)S(1)}, f32[128,512]{1,0:T(8,128)S(1)}, u32[]{:S(2)}, u32[]{:S(2)}) collective-permute-start(f32[128,512]{1,0:T(8,128)S(1)} %get-tuple-element.36.own0), channel_id=1, source_target_pairs={{0,8},{1,9},{3,2},{4,12},{6,5},{7,15},{8,0},{9,1},{11,10},{12,4},{... | collective-permute-start | bytes 786440 | tf_op jit(solution)/shard_map/ppermute | solution.py:222
  42.3 6.8 %collective-permute-start.12 = (f32[64,512]{1,0:T(8,128)S(1)}, f32[64,512]{1,0:T(8,128)S(1)}, u32[]{:S(2)}, u32[]{:S(2)}) collective-permute-start(f32[64,512]{1,0:T(8,128)S(1)} %get-tuple-element.47), channel_id=1, source_target_pairs={{0,1},{1,0},{2,10},{3,4},{4,3},{5,13},{6,7},{7,6},{8,9},{9,8},{10,... | collective-permute-start | bytes 393224 | tf_op jit(solution)/shard_map/ppermute | solution.py:222
  49.1 0.9 %shard_map.40 = (f32[64,512]{1,0:T(8,128)S(1)}, f32[64,512]{1,0:T(8,128)S(1)}) custom-call(s32[8]{0:T(128)S(1)} %copy-done.2, f32[128,256]{1,0:T(8,128)S(1)} %collective-permute-done.5.refs_1_, f32[128,256]{1,0:T(8,128)S(1)} %collective-permute-done.8.refs_2_, f32[64,512]{1,0:T(8,128)S(1)} %collective-permute-done.11.refs_3_, ...), custom_call_target="tpu_custom_call" | custom-call | tf_op jit(solution)/shard_map/pallas_call | solution.py:241
  50.1 2.5 %collective-permute-done.12.refs_3_ = f32[64,512]{1,0:T(8,128)S(1)} collective-permute-done((f32[64,512]{1,0:T(8,128)S(1)}, f32[64,512]{1,0:T(8,128)S(1)}, u32[]{:S(2)}, u32[]{:S(2)}) %collective-permute-start.12) | collective-permute-done | bytes 131104 | tf_op jit(solution)/shard_map/ppermute | solution.py:222
  52.7 0.9 %shard_map.41 = (f32[64,512]{1,0:T(8,128)S(1)}, f32[64,512]{1,0:T(8,128)S(1)}) custom-call(s32[8]{0:T(128)S(1)} %copy-done.2, f32[128,256]{1,0:T(8,128)S(1)} %collective-permute-done.5.refs_1_, f32[128,256]{1,0:T(8,128)S(1)} %collective-permute-done.8.refs_2_, f32[64,512]{1,0:T(8,128)S(1)} %collective-permute-done.12.refs_3_, ...), custom_call_target="tpu_custom_call" | custom-call | tf_op jit(solution)/shard_map/pallas_call | solution.py:241
  53.7 2.1 %collective-permute-start.24 = (f32[64,512]{1,0:T(8,128)S(1)}, f32[64,512]{1,0:T(8,128)S(1)}, u32[]{:S(2)}, u32[]{:S(2)}) collective-permute-start(f32[64,512]{1,0:T(8,128)S(1)} %get-tuple-element.48.refs_1_), channel_id=1, source_target_pairs={{0,8},{1,9},{2,4},{3,11},{4,2},{5,7},{6,14},{7,5},{8,0},{9,1},{10,... | collective-permute-start | bytes 393224 | tf_op jit(solution)/shard_map/ppermute | solution.py:222
  56.4 2.1 %collective-permute-done.20.refs_2_ = f32[64,512]{1,0:T(8,128)S(1)} collective-permute-done((f32[64,512]{1,0:T(8,128)S(1)}, f32[64,512]{1,0:T(8,128)S(1)}, u32[]{:S(2)}, u32[]{:S(2)}) %collective-permute-start.20) | collective-permute-done | bytes 131104 | tf_op jit(solution)/shard_map/ppermute | solution.py:222
  59.7 0.7 collective-permute-done.24.refs_2_
  61.1 5.8 %collective-permute-start.26 = (f32[64,512]{1,0:T(8,128)S(1)}, f32[64,512]{1,0:T(8,128)S(1)}, u32[]{:S(2)}, u32[]{:S(2)}) collective-permute-start(f32[64,512]{1,0:T(8,128)S(1)} %get-tuple-element.65), channel_id=1, source_target_pairs={{0,8},{1,9},{2,4},{3,11},{4,2},{5,7},{6,14},{7,5},{8,0},{9,1},{10,... | collective-permute-start | bytes 393224 | tf_op jit(solution)/shard_map/ppermute | solution.py:222
  66.9 7.1 %collective-permute-done.26.refs_6_ = f32[64,512]{1,0:T(8,128)S(1)} collective-permute-done((f32[64,512]{1,0:T(8,128)S(1)}, f32[64,512]{1,0:T(8,128)S(1)}, u32[]{:S(2)}, u32[]{:S(2)}) %collective-permute-start.26) | collective-permute-done | bytes 131104 | tf_op jit(solution)/shard_map/ppermute | solution.py:222
  74.1 1.5 %collective-permute-done.27.refs_7_ = f32[64,512]{1,0:T(8,128)S(1)} collective-permute-done((f32[64,512]{1,0:T(8,128)S(1)}, f32[64,512]{1,0:T(8,128)S(1)}, u32[]{:S(2)}, u32[]{:S(2)}) %collective-permute-start.27) | collective-permute-done | bytes 131104 | tf_op jit(solution)/shard_map/ppermute | solution.py:222
  75.5 0.7 shard_map.48
  (52 shorter events, 6.9 us)
Async XLA Ops:
  1.4 13.7 %collective-permute-start.3 = (f32[2,128,512]{2,1,0:T(8,128)S(1)}, f32[2,128,512]{2,1,0:T(8,128)S(1)}, u32[]{:S(2)}, u32[]{:S(2)}) collective-permute-start(f32[2,128,512]{2,1,0:T(8,128)S(1)} %get-tuple-element.68), channel_id=1, source_target_pairs={{0,16},{1,17},{2,18},{3,19},{4,20},{5,21},{6,22},{7,23},{8,24},{9,... | collective-permute-start | bytes 1572872 | tf_op jit(solution)/shard_map/ppermute | solution.py:230
  2.9 12.2 %collective-permute-start.15 = (f32[2,128,512]{2,1,0:T(8,128)S(1)}, f32[2,128,512]{2,1,0:T(8,128)S(1)}, u32[]{:S(2)}, u32[]{:S(2)}) collective-permute-start(f32[2,128,512]{2,1,0:T(8,128)S(1)} %get-tuple-element.67), channel_id=1, source_target_pairs={{0,8},{1,2},{3,11},{4,5},{6,14},{7,15},{8,0},{9,10},{11,3},{12,13}... | collective-permute-start | bytes 1572872 | tf_op jit(solution)/shard_map/ppermute | solution.py:222
  4.9 13.8 %collective-permute-start.2 = (f32[4,128,512]{2,1,0:T(8,128)S(1)}, f32[4,128,512]{2,1,0:T(8,128)S(1)}, u32[]{:S(2)}, u32[]{:S(2)}) collective-permute-start(f32[4,128,512]{2,1,0:T(8,128)S(1)} %bitcast.9), channel_id=1, source_target_pairs={{0,8},{8,0},{16,24},{24,16},{1,9},{9,1},{17,25},{25,17},{2,10},{10... | collective-permute-start | bytes 3145736 | tf_op jit(solution)/shard_map/ppermute | solution.py:235
  5.4 10.2 %collective-permute-start = (f32[128,512]{1,0:T(8,128)S(1)}, f32[128,512]{1,0:T(8,128)S(1)}, u32[]{:S(2)}, u32[]{:S(2)}) collective-permute-start(f32[128,512]{1,0:T(8,128)S(1)} %copy-done.1), channel_id=1, source_target_pairs={{0,1},{1,0},{2,10},{3,4},{4,3},{5,13},{6,7},{7,6},{8,9},{9,8},{10,... | collective-permute-start | bytes 786440 | tf_op jit(solution)/shard_map/ppermute | solution.py:222
  5.9 9.8 %collective-permute-start.1 = (f32[128,512]{1,0:T(8,128)S(1)}, f32[128,512]{1,0:T(8,128)S(1)}, u32[]{:S(2)}, u32[]{:S(2)}) collective-permute-start(f32[128,512]{1,0:T(8,128)S(1)} %copy-done.1), channel_id=1, source_target_pairs={{0,2},{1,9},{2,0},{3,5},{4,12},{5,3},{6,14},{7,15},{8,10},{9,1},{1... | collective-permute-start | bytes 786440 | tf_op jit(solution)/shard_map/ppermute | solution.py:222
  15.1 4.1 %collective-permute-start.17 = (f32[2,128,512]{2,1,0:T(8,128)S(1)}, f32[2,128,512]{2,1,0:T(8,128)S(1)}, u32[]{:S(2)}, u32[]{:S(2)}) collective-permute-start(f32[2,128,512]{2,1,0:T(8,128)S(1)} %collective-permute-done.15.refs_0_.refs_4_), channel_id=1, source_target_pairs={{0,8},{1,9},{2,18},{3,11},{4,12},{5,21},{6,14},{7,15},{8,0},{9,1},... | collective-permute-start | bytes 1572872 | tf_op jit(solution)/shard_map/ppermute | solution.py:230
  18.5 14.4 %collective-permute-start.7 = (f32[1,128,512]{2,1,0:T(8,128)S(1)}, f32[1,128,512]{2,1,0:T(8,128)S(1)}, u32[]{:S(2)}, u32[]{:S(2)}) collective-permute-start(f32[1,128,512]{2,1,0:T(8,128)S(1)} %collective-permute-done.6.refs_4_.refs_2_), channel_id=1, source_target_pairs={{0,8},{8,0},{16,24},{24,16},{1,9},{9,1},{17,25},{25,17},{2,10},{10... | collective-permute-start | bytes 786440 | tf_op jit(solution)/shard_map/ppermute | solution.py:235
  18.7 14.9 %collective-permute-start.10 = (f32[1,128,512]{2,1,0:T(8,128)S(1)}, f32[1,128,512]{2,1,0:T(8,128)S(1)}, u32[]{:S(2)}, u32[]{:S(2)}) collective-permute-start(f32[1,128,512]{2,1,0:T(8,128)S(1)} %collective-permute-done.9.refs_4_), channel_id=1, source_target_pairs={{0,8},{8,0},{16,24},{24,16},{1,9},{9,1},{17,25},{25,17},{2,10},{10... | collective-permute-start | bytes 786440 | tf_op jit(solution)/shard_map/ppermute | solution.py:235
  19.0 34.5 %collective-permute-start.16 = (f32[2,128,512]{2,1,0:T(8,128)S(1)}, f32[2,128,512]{2,1,0:T(8,128)S(1)}, u32[]{:S(2)}, u32[]{:S(2)}) collective-permute-start(f32[2,128,512]{2,1,0:T(8,128)S(1)} %collective-permute-done.15.refs_0_.refs_4_), channel_id=1, source_target_pairs={{0,8},{8,0},{16,24},{24,16},{1,9},{9,1},{17,25},{25,17},{2,10},{10... | collective-permute-start | bytes 1572872 | tf_op jit(solution)/shard_map/ppermute | solution.py:235
  19.2 34.5 %collective-permute-start.18 = (f32[2,128,512]{2,1,0:T(8,128)S(1)}, f32[2,128,512]{2,1,0:T(8,128)S(1)}, u32[]{:S(2)}, u32[]{:S(2)}) collective-permute-start(f32[2,128,512]{2,1,0:T(8,128)S(1)} %collective-permute-done.17.refs_2_.refs_6_), channel_id=1, source_target_pairs={{0,8},{8,0},{16,24},{24,16},{1,9},{9,1},{17,25},{25,17},{2,10},{10... | collective-permute-start | bytes 1572872 | tf_op jit(solution)/shard_map/ppermute | solution.py:235
  20.5 16.4 %collective-permute-start.5 = (f32[128,256]{1,0:T(8,128)S(1)}, f32[128,256]{1,0:T(8,128)S(1)}, u32[]{:S(2)}, u32[]{:S(2)}) collective-permute-start(f32[128,256]{1,0:T(8,128)S(1)} %get-tuple-element.37), channel_id=1, source_target_pairs={{0,1},{1,0},{2,10},{3,4},{4,3},{5,13},{6,7},{7,6},{8,9},{9,8},{10,... | collective-permute-start | bytes 393224 | tf_op jit(solution)/shard_map/ppermute | solution.py:222
  33.0 17.1 %collective-permute-start.22 = (f32[1,128,512]{2,1,0:T(8,128)S(1)}, f32[1,128,512]{2,1,0:T(8,128)S(1)}, u32[]{:S(2)}, u32[]{:S(2)}) collective-permute-start(f32[1,128,512]{2,1,0:T(8,128)S(1)} %collective-permute-done.21.refs_6_), channel_id=1, source_target_pairs={{0,8},{8,0},{16,24},{24,16},{1,9},{9,1},{17,25},{25,17},{2,10},{10... | collective-permute-start | bytes 786440 | tf_op jit(solution)/shard_map/ppermute | solution.py:235
  33.5 6.4 %collective-permute-start.8 = (f32[128,256]{1,0:T(8,128)S(1)}, f32[128,256]{1,0:T(8,128)S(1)}, u32[]{:S(2)}, u32[]{:S(2)}) collective-permute-start(f32[128,256]{1,0:T(8,128)S(1)} %get-tuple-element.39), channel_id=1, source_target_pairs={{0,1},{1,0},{2,10},{3,4},{4,3},{5,13},{6,7},{7,6},{8,9},{9,8},{10,... | collective-permute-start | bytes 393224 | tf_op jit(solution)/shard_map/ppermute | solution.py:222
  36.8 5.5 %collective-permute-start.11 = (f32[64,512]{1,0:T(8,128)S(1)}, f32[64,512]{1,0:T(8,128)S(1)}, u32[]{:S(2)}, u32[]{:S(2)}) collective-permute-start(f32[64,512]{1,0:T(8,128)S(1)} %get-tuple-element.41), channel_id=1, source_target_pairs={{0,1},{1,0},{2,10},{3,4},{4,3},{5,13},{6,7},{7,6},{8,9},{9,8},{10,... | collective-permute-start | bytes 393224 | tf_op jit(solution)/shard_map/ppermute | solution.py:222
  40.0 15.8 %collective-permute-start.14 = (f32[128,512]{1,0:T(8,128)S(1)}, f32[128,512]{1,0:T(8,128)S(1)}, u32[]{:S(2)}, u32[]{:S(2)}) collective-permute-start(f32[128,512]{1,0:T(8,128)S(1)} %get-tuple-element.36.own0), channel_id=1, source_target_pairs={{0,8},{1,9},{3,2},{4,12},{6,5},{7,15},{8,0},{9,1},{11,10},{12,4},{... | collective-permute-start | bytes 786440 | tf_op jit(solution)/shard_map/ppermute | solution.py:222
  42.3 10.3 %collective-permute-start.12 = (f32[64,512]{1,0:T(8,128)S(1)}, f32[64,512]{1,0:T(8,128)S(1)}, u32[]{:S(2)}, u32[]{:S(2)}) collective-permute-start(f32[64,512]{1,0:T(8,128)S(1)} %get-tuple-element.47), channel_id=1, source_target_pairs={{0,1},{1,0},{2,10},{3,4},{4,3},{5,13},{6,7},{7,6},{8,9},{9,8},{10,... | collective-permute-start | bytes 393224 | tf_op jit(solution)/shard_map/ppermute | solution.py:222
  50.1 5.8 %collective-permute-start.13 = (f32[64,512]{1,0:T(8,128)S(1)}, f32[64,512]{1,0:T(8,128)S(1)}, u32[]{:S(2)}, u32[]{:S(2)}) collective-permute-start(f32[64,512]{1,0:T(8,128)S(1)} %get-tuple-element.49), channel_id=1, source_target_pairs={{0,8},{1,2},{2,1},{3,11},{4,5},{5,4},{6,14},{7,15},{8,0},{9,10},{1... | collective-permute-start | bytes 393224 | tf_op jit(solution)/shard_map/ppermute | solution.py:222
  52.7 5.8 %collective-permute-start.20 = (f32[64,512]{1,0:T(8,128)S(1)}, f32[64,512]{1,0:T(8,128)S(1)}, u32[]{:S(2)}, u32[]{:S(2)}) collective-permute-start(f32[64,512]{1,0:T(8,128)S(1)} %get-tuple-element.46.refs_0_), channel_id=1, source_target_pairs={{0,8},{1,9},{2,4},{3,11},{4,2},{5,7},{6,14},{7,5},{8,0},{9,1},{10,... | collective-permute-start | bytes 393224 | tf_op jit(solution)/shard_map/ppermute | solution.py:222
  53.6 5.6 %collective-permute-start.19 = (f32[64,512]{1,0:T(8,128)S(1)}, f32[64,512]{1,0:T(8,128)S(1)}, u32[]{:S(2)}, u32[]{:S(2)}) collective-permute-start(f32[64,512]{1,0:T(8,128)S(1)} %get-tuple-element.55), channel_id=1, source_target_pairs={{0,8},{1,2},{2,1},{3,11},{4,5},{5,4},{6,14},{7,15},{8,0},{9,10},{1... | collective-permute-start | bytes 393224 | tf_op jit(solution)/shard_map/ppermute | solution.py:222
  53.7 6.8 %collective-permute-start.24 = (f32[64,512]{1,0:T(8,128)S(1)}, f32[64,512]{1,0:T(8,128)S(1)}, u32[]{:S(2)}, u32[]{:S(2)}) collective-permute-start(f32[64,512]{1,0:T(8,128)S(1)} %get-tuple-element.48.refs_1_), channel_id=1, source_target_pairs={{0,8},{1,9},{2,4},{3,11},{4,2},{5,7},{6,14},{7,5},{8,0},{9,1},{10,... | collective-permute-start | bytes 393224 | tf_op jit(solution)/shard_map/ppermute | solution.py:222
  59.1 7.9 %collective-permute-start.23 = (f32[64,512]{1,0:T(8,128)S(1)}, f32[64,512]{1,0:T(8,128)S(1)}, u32[]{:S(2)}, u32[]{:S(2)}) collective-permute-start(f32[64,512]{1,0:T(8,128)S(1)} %get-tuple-element.62), channel_id=1, source_target_pairs={{0,8},{1,9},{2,3},{3,2},{4,12},{5,6},{6,5},{7,15},{8,0},{9,1},{10,... | collective-permute-start | bytes 393224 | tf_op jit(solution)/shard_map/ppermute | solution.py:222
  61.0 5.9 %collective-permute-start.25 = (f32[64,512]{1,0:T(8,128)S(1)}, f32[64,512]{1,0:T(8,128)S(1)}, u32[]{:S(2)}, u32[]{:S(2)}) collective-permute-start(f32[64,512]{1,0:T(8,128)S(1)} %get-tuple-element.64), channel_id=1, source_target_pairs={{0,8},{1,9},{2,3},{3,2},{4,12},{5,6},{6,5},{7,15},{8,0},{9,1},{10,... | collective-permute-start | bytes 393224 | tf_op jit(solution)/shard_map/ppermute | solution.py:222
  61.1 13.0 %collective-permute-start.26 = (f32[64,512]{1,0:T(8,128)S(1)}, f32[64,512]{1,0:T(8,128)S(1)}, u32[]{:S(2)}, u32[]{:S(2)}) collective-permute-start(f32[64,512]{1,0:T(8,128)S(1)} %get-tuple-element.65), channel_id=1, source_target_pairs={{0,8},{1,9},{2,4},{3,11},{4,2},{5,7},{6,14},{7,5},{8,0},{9,1},{10,... | collective-permute-start | bytes 393224 | tf_op jit(solution)/shard_map/ppermute | solution.py:222
  66.9 8.6 %collective-permute-start.27 = (f32[64,512]{1,0:T(8,128)S(1)}, f32[64,512]{1,0:T(8,128)S(1)}, u32[]{:S(2)}, u32[]{:S(2)}) collective-permute-start(f32[64,512]{1,0:T(8,128)S(1)} %get-tuple-element.66), channel_id=1, source_target_pairs={{0,8},{1,9},{2,4},{3,11},{4,2},{5,7},{6,14},{7,5},{8,0},{9,1},{10,... | collective-permute-start | bytes 393224 | tf_op jit(solution)/shard_map/ppermute | solution.py:222
  (7 other events, 25.6 us)
where the time goes:
time: 76.5 us; the launch traced here: 76.3 us
  starting transfers between devices  39 us (51%)
  waiting for transfers between devices  28.8 us (38%)
  Pallas kernels  6.78 us (9%)
  local copies, waits for them, and re-layouts  1.42 us (2%)
    ppermute x16, starting transfers between devices, along(): return lax.ppermute(array, ('row', 'col'), pairs)  34.6 us
    ppermute x16, waiting for transfers between devices, along(): return lax.ppermute(array, ('row', 'col'), pairs)  17.5 us
    ppermute x5, waiting for transfers between devices, across(): return lax.ppermute(array, ('row', 'col'), pairs)  11.3 us
    pallas_call x12, Pallas kernels, call(): pl.pallas_call(kernel, out_shape=outs, in_specs=[scalars if op.dtype == j...  6.78 us
    ppermute x5, starting transfers between devices, across(): return lax.ppermute(array, ('row', 'col'), pairs)  2.76 us
    ppermute x7, starting transfers between devices, spread(): lax.ppermute(pieces[mask], 'row', [(i, i ^ bit) for i in range(ring)])  1.59 us
  transfers between devices with their start and end apart: 28, of which 11 were waited for; matrix products, arithmetic and copies ran while one was open for 0% of the time, Pallas kernels for 8%

commit v1 on v0

--- a/solution.py
+++ b/solution.py
@@ -134,9 +134,10 @@
 
 def last_kernel(groups, part, turns, stride, *refs):
     count, half = len(turns), FACTORS // 2
-    offsets_ref, first, second = refs[:3]
-    weights = refs[3 : 3 + 2 * count]
-    *results, buf = refs[3 + 2 * count :]
+    places = 3 if count == FACTORS + half else 2
+    offsets_ref, *blocks = refs[: 1 + places]
+    weights = refs[1 + places : 1 + places + 2 * count]
+    *results, buf = refs[1 + places + 2 * count :]
     column, tick, offset, last = place(groups, offsets_ref)
     before = offsets_ref[jnp.maximum(column - 1, 0)]
 
@@ -144,11 +145,9 @@
 
     @pl.when(tick == TICKS - 1)
     def _():
-        buf[:, : 2 * stride] = first[...]
-        if second.shape[0] == height:
-            buf[:, 2 * stride :] = second[...]
-        else:
-            buf[:, 2 * stride :] = second[part * height : (part + 1) * height]
+        for i, block in enumerate(blocks):
+            first = part * height if block.shape[0] > height else 0
+            buf[:, 2 * i * stride : 2 * (i + 1) * stride] = block[first : first + height]
         for i, turn in enumerate(turns):
             if turn < half:
                 start = before + turn
@@ -162,8 +161,8 @@
                 here = strips(start, 2, stride)
                 buf[here] = product(buf[here], weights[2 * i], weights[2 * i + 1])
 
-        results[0][...] = buf[:, : 2 * stride]
-        results[1][...] = buf[:, 2 * stride :]
+        for i, result in enumerate(results):
+            result[...] = buf[:, 2 * i * stride : 2 * (i + 1) * stride]
 
 
 def pick_kernel(own0, *refs):
@@ -180,7 +179,8 @@
         (
             (tick == 1) & (column < TICKS),
             tick == 2,
-            (tick == 0) & (column >= TICKS),
+            (tick == 0) & (column >= TICKS) & (lax.rem(column, 2) == 1),
+            (tick == 0) & (column >= TICKS) & (lax.rem(column, 2) == 0),
             (tick == 1) & (column >= TICKS),
         )
     ):
@@ -208,6 +208,9 @@
             for i in range(groups)
             if i % TICKS == tick and 0 <= i + distance < groups
         }
+        return trade(array, swaps, back)
+
+    def trade(array, swaps, back=True):
         moves = {i: i for i in range(groups)}
         for source, target in swaps.items():
             moves |= {source: target, target: source}
@@ -254,6 +257,7 @@
         return [block(order, bf16, order)] * (2 * count)
 
     half = FACTORS // 2
+    kinds = [[i for i in range(groups) if i % TICKS == tick] for tick in range(TICKS)]
     whole = factors[0]
     own = spread({0: whole})
     away = {
@@ -299,7 +303,7 @@
     last_pairs = ready(((2, 0), (3, 0)), *gathered[2], *mine)
     low = block(high=rows // 2)
     buf = pltpu.VMEM((rows // 2, 2 * width), f32)
-    own1, onward, fourth, own2, near, far = [], [], [], [], [], []
+    own1, onward, fourth = [], [], []
     for i in range(2):
         kept, sent = call(
             functools.partial(middle_kernel, groups, i, stride),
@@ -314,30 +318,34 @@
         own1.append(kept)
         onward.append(along(sent, 1, 1))
         fourth.append(along(kept, -2, 1))
-    for i in range(2):
-        kept, sent = call(
-            functools.partial(last_kernel, groups, i, (0, 1, 2, 3), stride),
-            [low] * 2,
-            [buf],
+
+    def finish(part, turns, blocks, weights):
+        return call(
+            functools.partial(last_kernel, groups, part, turns, stride),
+            [low] * len(blocks),
+            [pltpu.VMEM((rows // 2, len(blocks) * width), f32)],
             offsets,
-            onward[i],
-            third,
-            *handed_pairs,
-            *first_pairs,
+            *blocks,
+            *weights,
         )
-        own2.append(kept)
-        next_block, after = call(
-            functools.partial(last_kernel, groups, i, (4, 5), stride),
-            [low] * 2,
-            [buf],
-            offsets,
-            sent,
-            fourth[i],
-            *last_pairs,
-        )
-        near.append(along(next_block, 1, 2))
-        far.append(along(after, 2, 2))
-    (out,) = call(pick_kernel, [block()], [], own0, *own1, *own2, *near, *far)
+
+    early_turns = [*handed_pairs, *first_pairs]
+    kept, sent = finish(0, (0, 1, 2, 3), [onward[0], third], early_turns)
+    own2 = [kept]
+    near, far = finish(0, (4, 5), [sent, fourth[0]], last_pairs)
+    lasts = [i for i in kinds[2] if i + 1 < groups]
+    near0 = trade(near, {i: i - 1 if i % 2 else i + 1 for i in lasts})
+    far0 = along(far, 2, 2)
+    kept, near, far = finish(
+        1, (0, 1, 2, 3, 4, 5), [onward[1], third, fourth[1]], early_turns + list(last_pairs)
+    )
+    own2.append(kept)
+    near1 = along(near, 1, 2)
+    far1 = along(far, 2, 2)
+    relayed = trade(near0, {i - 1: i + 1 for i in lasts if i % 2}, False)
+    (out,) = call(
+        pick_kernel, [block()], [], own0, *own1, *own2, near0, near1, relayed, near1, far0, far1
+    )
     return out
 
 

time: 76.5 us -> 75 us (0.980)
  starting transfers between devices: 39 us -> 37 us
  waiting for transfers between devices: 28.8 us -> 29.9 us
    ppermute x5, waiting for transfers between devices: 11.3 us -> 13.4 us  [across(): return lax.ppermute(array, ('row', 'col'), pairs)]
    ppermute x16 -> x17, starting transfers between devices: 34.6 us -> 32.9 us  [trade(): return lax.ppermute(array, ('row', 'col'), pairs)]
    ppermute x16 -> x17, waiting for transfers between devices: 17.5 us -> 16.5 us  [trade(): return lax.ppermute(array, ('row', 'col'), pairs)]
    pallas_call x12 -> x11, Pallas kernels: 6.78 us -> 6.23 us  [call(): pl.pallas_call(kernel, out_shape=outs, in_specs=[scalars if op.dtype == j...]
  transfers between devices with their start and end apart: 28 -> 29, of which waited for: 11 -> 11; matrix products, arithmetic and copies ran while one was open for 0% -> 0% of each run, Pallas kernels for 8% -> 7%
where the time goes in v1:
time: 75 us; the launch traced here: 74.8 us
  starting transfers between devices  37 us (49%)
  waiting for transfers between devices  29.9 us (40%)
  Pallas kernels  6.23 us (8%)
  local copies, waits for them, and re-layouts  1.43 us (2%)
    ppermute x17, starting transfers between devices, trade(): return lax.ppermute(array, ('row', 'col'), pairs)  32.9 us
    ppermute x17, waiting for transfers between devices, trade(): return lax.ppermute(array, ('row', 'col'), pairs)  16.5 us
    ppermute x5, waiting for transfers between devices, across(): return lax.ppermute(array, ('row', 'col'), pairs)  13.4 us
    pallas_call x11, Pallas kernels, call(): pl.pallas_call(kernel, out_shape=outs, in_specs=[scalars if op.dtype == j...  6.23 us
    ppermute x5, starting transfers between devices, across(): return lax.ppermute(array, ('row', 'col'), pairs)  2.85 us
  transfers between devices with their start and end apart: 29, of which 11 were waited for; matrix products, arithmetic and copies ran while one was open for 0% of the time, Pallas kernels for 7%

profile of v1, /device:TPU:28, one launch (start us, length us, event | category | flops | bytes accessed | tf_op | source)
XLA Modules:
  0.0 74.8 jit_solution(4019987234484716551)
XLA Ops:
  0.0 1.4 %slice_bitcast_fusion = (f32[2,128,512]{2,1,0:T(8,128)S(1)}, f32[2,128,512]{2,1,0:T(8,128)S(1)}) fusion(f32[1,4,128,512]{3,2,1,0:T(8,128)} %param.4), kind=kLoop, calls=%fused_computation | loop fusion | bytes 2097152 | tf_op jit(solution)/shard_map/slice | solution.py:269
  1.4 1.9 %collective-permute-start.15 = (f32[2,128,512]{2,1,0:T(8,128)S(1)}, f32[2,128,512]{2,1,0:T(8,128)S(1)}, u32[]{:S(2)}, u32[]{:S(2)}) collective-permute-start(f32[2,128,512]{2,1,0:T(8,128)S(1)} %get-tuple-element.65), channel_id=1, source_target_pairs={{0,8},{1,2},{3,11},{4,5},{6,14},{7,15},{8,0},{9,10},{11,3},{12,13}... | collective-permute-start | bytes 1572872 | tf_op jit(solution)/shard_map/ppermute | solution.py:225
  3.3 1.6 %collective-permute-start.3 = (f32[2,128,512]{2,1,0:T(8,128)S(1)}, f32[2,128,512]{2,1,0:T(8,128)S(1)}, u32[]{:S(2)}, u32[]{:S(2)}) collective-permute-start(f32[2,128,512]{2,1,0:T(8,128)S(1)} %get-tuple-element.66), channel_id=1, source_target_pairs={{0,16},{1,17},{2,18},{3,19},{4,20},{5,21},{6,22},{7,23},{8,24},{9,... | collective-permute-start | bytes 1572872 | tf_op jit(solution)/shard_map/ppermute | solution.py:233
  6.1 11.6 %collective-permute-done.3.refs_6_ = f32[2,128,512]{2,1,0:T(8,128)S(1)} collective-permute-done((f32[2,128,512]{2,1,0:T(8,128)S(1)}, f32[2,128,512]{2,1,0:T(8,128)S(1)}, u32[]{:S(2)}, u32[]{:S(2)}) %collective-permute-start.3) | collective-permute-done | bytes 524320 | tf_op jit(solution)/shard_map/ppermute | solution.py:233
  17.8 0.6 collective-permute-start.6
  18.4 1.6 %collective-permute-done.6.refs_4_.refs_2_ = f32[1,128,512]{2,1,0:T(8,128)S(1)} collective-permute-done((f32[1,128,512]{2,1,0:T(8,128)S(1)}, f32[1,128,512]{2,1,0:T(8,128)S(1)}, u32[]{:S(2)}, u32[]{:S(2)}) %collective-permute-start.6) | collective-permute-done | bytes 262176 | tf_op jit(solution)/shard_map/ppermute | solution.py:233
  21.4 0.9 %shard_map.37 = (f32[128,512]{1,0:T(8,128)S(1)}, f32[128,1024]{1,0:T(8,128)S(1)}, f32[128,256]{1,0:T(8,128)S(1)}, bf16[512,512]{1,0:T(8,128)(2,1)S(1)}, bf16[512...) custom-call(s32[8]{0:T(128)S(1)} %copy-done.2, f32[128,512]{1,0:T(8,128)S(1)} %copy-done.1, ...), custom_call_target="tpu_custom_call" | custom-call | tf_op jit(solution)/shard_map/pallas_call | solution.py:244
  22.3 13.2 %collective-permute-start.5 = (f32[128,256]{1,0:T(8,128)S(1)}, f32[128,256]{1,0:T(8,128)S(1)}, u32[]{:S(2)}, u32[]{:S(2)}) collective-permute-start(f32[128,256]{1,0:T(8,128)S(1)} %get-tuple-element.36), channel_id=1, source_target_pairs={{0,1},{1,0},{2,10},{3,4},{4,3},{5,13},{6,7},{7,6},{8,9},{9,8},{10,... | collective-permute-start | bytes 393224 | tf_op jit(solution)/shard_map/ppermute | solution.py:225
  37.0 2.4 %collective-permute-done.5.refs_1_ = f32[128,256]{1,0:T(8,128)S(1)} collective-permute-done((f32[128,256]{1,0:T(8,128)S(1)}, f32[128,256]{1,0:T(8,128)S(1)}, u32[]{:S(2)}, u32[]{:S(2)}) %collective-permute-start.5) | collective-permute-done | bytes 131104 | tf_op jit(solution)/shard_map/ppermute | solution.py:225
  39.4 2.5 %collective-permute-start.8 = (f32[128,256]{1,0:T(8,128)S(1)}, f32[128,256]{1,0:T(8,128)S(1)}, u32[]{:S(2)}, u32[]{:S(2)}) collective-permute-start(f32[128,256]{1,0:T(8,128)S(1)} %get-tuple-element.38), channel_id=1, source_target_pairs={{0,1},{1,0},{2,10},{3,4},{4,3},{5,13},{6,7},{7,6},{8,9},{9,8},{10,... | collective-permute-start | bytes 393224 | tf_op jit(solution)/shard_map/ppermute | solution.py:225
  41.9 1.3 %collective-permute-done.11.refs_3_ = f32[64,512]{1,0:T(8,128)S(1)} collective-permute-done((f32[64,512]{1,0:T(8,128)S(1)}, f32[64,512]{1,0:T(8,128)S(1)}, u32[]{:S(2)}, u32[]{:S(2)}) %collective-permute-start.11) | collective-permute-done | bytes 131104 | tf_op jit(solution)/shard_map/ppermute | solution.py:225
  43.2 1.9 %collective-permute-start.14 = (f32[128,512]{1,0:T(8,128)S(1)}, f32[128,512]{1,0:T(8,128)S(1)}, u32[]{:S(2)}, u32[]{:S(2)}) collective-permute-start(f32[128,512]{1,0:T(8,128)S(1)} %get-tuple-element.35.own0), channel_id=1, source_target_pairs={{0,8},{1,9},{3,2},{4,12},{6,5},{7,15},{8,0},{9,1},{11,10},{12,4},{... | collective-permute-start | bytes 786440 | tf_op jit(solution)/shard_map/ppermute | solution.py:225
  45.5 3.2 %collective-permute-start.12 = (f32[64,512]{1,0:T(8,128)S(1)}, f32[64,512]{1,0:T(8,128)S(1)}, u32[]{:S(2)}, u32[]{:S(2)}) collective-permute-start(f32[64,512]{1,0:T(8,128)S(1)} %get-tuple-element.46), channel_id=1, source_target_pairs={{0,1},{1,0},{2,10},{3,4},{4,3},{5,13},{6,7},{7,6},{8,9},{9,8},{10,... | collective-permute-start | bytes 393224 | tf_op jit(solution)/shard_map/ppermute | solution.py:225
  48.7 0.9 %shard_map.40 = (f32[64,512]{1,0:T(8,128)S(1)}, f32[64,512]{1,0:T(8,128)S(1)}) custom-call(s32[8]{0:T(128)S(1)} %copy-done.2, f32[128,256]{1,0:T(8,128)S(1)} %collective-permute-done.5.refs_1_, f32[128,256]{1,0:T(8,128)S(1)} %collective-permute-done.8.refs_2_, f32[64,512]{1,0:T(8,128)S(1)} %collective-permute-done.11.refs_3_, ...), custom_call_target="tpu_custom_call" | custom-call | tf_op jit(solution)/shard_map/pallas_call | solution.py:244
  49.7 2.5 %collective-permute-done.12.refs_3_ = f32[64,512]{1,0:T(8,128)S(1)} collective-permute-done((f32[64,512]{1,0:T(8,128)S(1)}, f32[64,512]{1,0:T(8,128)S(1)}, u32[]{:S(2)}, u32[]{:S(2)}) %collective-permute-start.12) | collective-permute-done | bytes 131104 | tf_op jit(solution)/shard_map/ppermute | solution.py:225
  52.3 0.9 %shard_map.41 = (f32[64,512]{1,0:T(8,128)S(1)}, f32[64,512]{1,0:T(8,128)S(1)}) custom-call(s32[8]{0:T(128)S(1)} %copy-done.2, f32[128,256]{1,0:T(8,128)S(1)} %collective-permute-done.5.refs_1_, f32[128,256]{1,0:T(8,128)S(1)} %collective-permute-done.8.refs_2_, f32[64,512]{1,0:T(8,128)S(1)} %collective-permute-done.12.refs_3_, ...), custom_call_target="tpu_custom_call" | custom-call | tf_op jit(solution)/shard_map/pallas_call | solution.py:244
  53.3 2.8 %collective-permute-start.20 = (f32[64,512]{1,0:T(8,128)S(1)}, f32[64,512]{1,0:T(8,128)S(1)}, u32[]{:S(2)}, u32[]{:S(2)}) collective-permute-start(f32[64,512]{1,0:T(8,128)S(1)} %get-tuple-element.47.refs_1_), channel_id=1, source_target_pairs={{0,8},{1,9},{2,4},{3,11},{4,2},{5,7},{6,14},{7,5},{8,0},{9,1},{10,... | collective-permute-start | bytes 393224 | tf_op jit(solution)/shard_map/ppermute | solution.py:225
  56.6 1.5 %collective-permute-done.23.refs_2_ = f32[64,512]{1,0:T(8,128)S(1)} collective-permute-done((f32[64,512]{1,0:T(8,128)S(1)}, f32[64,512]{1,0:T(8,128)S(1)}, u32[]{:S(2)}, u32[]{:S(2)}) %collective-permute-start.23) | collective-permute-done | bytes 131104 | tf_op jit(solution)/shard_map/ppermute | solution.py:225
  58.8 1.3 %collective-permute-done.20.refs_3_ = f32[64,512]{1,0:T(8,128)S(1)} collective-permute-done((f32[64,512]{1,0:T(8,128)S(1)}, f32[64,512]{1,0:T(8,128)S(1)}, u32[]{:S(2)}, u32[]{:S(2)}) %collective-permute-start.20) | collective-permute-done | bytes 131104 | tf_op jit(solution)/shard_map/ppermute | solution.py:225
  60.7 4.3 %collective-permute-start.28 = (f32[64,512]{1,0:T(8,128)S(1)}, f32[64,512]{1,0:T(8,128)S(1)}, u32[]{:S(2)}, u32[]{:S(2)}) collective-permute-start(f32[64,512]{1,0:T(8,128)S(1)} %get-tuple-element.64), channel_id=1, source_target_pairs={{0,8},{1,9},{2,4},{3,11},{4,2},{5,7},{6,14},{7,5},{8,0},{9,1},{10,... | collective-permute-start | bytes 393224 | tf_op jit(solution)/shard_map/ppermute | solution.py:225
  65.0 1.9 %collective-permute-start.26 = (f32[64,512]{1,0:T(8,128)S(1)}, f32[64,512]{1,0:T(8,128)S(1)}, u32[]{:S(2)}, u32[]{:S(2)}) collective-permute-start(f32[64,512]{1,0:T(8,128)S(1)} %collective-permute-done.24.refs_4_), channel_id=1, source_target_pairs={{0,8},{1,9},{2,10},{3,11},{4,6},{5,13},{7,15},{8,0},{9,1},{10,2},{... | collective-permute-start | bytes 393224 | tf_op jit(solution)/shard_map/ppermute | solution.py:225
  67.0 5.1 %collective-permute-done.28.refs_9_ = f32[64,512]{1,0:T(8,128)S(1)} collective-permute-done((f32[64,512]{1,0:T(8,128)S(1)}, f32[64,512]{1,0:T(8,128)S(1)}, u32[]{:S(2)}, u32[]{:S(2)}) %collective-permute-start.28) | collective-permute-done | bytes 131104 | tf_op jit(solution)/shard_map/ppermute | solution.py:225
  72.0 2.1 %collective-permute-done.27.refs_8_ = f32[64,512]{1,0:T(8,128)S(1)} collective-permute-done((f32[64,512]{1,0:T(8,128)S(1)}, f32[64,512]{1,0:T(8,128)S(1)}, u32[]{:S(2)}, u32[]{:S(2)}) %collective-permute-start.27) | collective-permute-done | bytes 131104 | tf_op jit(solution)/shard_map/ppermute | solution.py:225
  74.1 0.7 shard_map.47
  (53 shorter events, 6.7 us)
Async XLA Ops:
  3.3 14.4 %collective-permute-start.3 = (f32[2,128,512]{2,1,0:T(8,128)S(1)}, f32[2,128,512]{2,1,0:T(8,128)S(1)}, u32[]{:S(2)}, u32[]{:S(2)}) collective-permute-start(f32[2,128,512]{2,1,0:T(8,128)S(1)} %get-tuple-element.66), channel_id=1, source_target_pairs={{0,16},{1,17},{2,18},{3,19},{4,20},{5,21},{6,22},{7,23},{8,24},{9,... | collective-permute-start | bytes 1572872 | tf_op jit(solution)/shard_map/ppermute | solution.py:233
  4.9 16.2 %collective-permute-start.2 = (f32[4,128,512]{2,1,0:T(8,128)S(1)}, f32[4,128,512]{2,1,0:T(8,128)S(1)}, u32[]{:S(2)}, u32[]{:S(2)}) collective-permute-start(f32[4,128,512]{2,1,0:T(8,128)S(1)} %bitcast.9), channel_id=1, source_target_pairs={{0,8},{8,0},{16,24},{24,16},{1,9},{9,1},{17,25},{25,17},{2,10},{10... | collective-permute-start | bytes 3145736 | tf_op jit(solution)/shard_map/ppermute | solution.py:238
  5.1 12.7 %collective-permute-start = (f32[128,512]{1,0:T(8,128)S(1)}, f32[128,512]{1,0:T(8,128)S(1)}, u32[]{:S(2)}, u32[]{:S(2)}) collective-permute-start(f32[128,512]{1,0:T(8,128)S(1)} %copy-done.1), channel_id=1, source_target_pairs={{0,1},{1,0},{2,10},{3,4},{4,3},{5,13},{6,7},{7,6},{8,9},{9,8},{10,... | collective-permute-start | bytes 786440 | tf_op jit(solution)/shard_map/ppermute | solution.py:225
  5.6 12.7 %collective-permute-start.1 = (f32[128,512]{1,0:T(8,128)S(1)}, f32[128,512]{1,0:T(8,128)S(1)}, u32[]{:S(2)}, u32[]{:S(2)}) collective-permute-start(f32[128,512]{1,0:T(8,128)S(1)} %copy-done.1), channel_id=1, source_target_pairs={{0,2},{1,9},{2,0},{3,5},{4,12},{5,3},{6,14},{7,15},{8,10},{9,1},{1... | collective-permute-start | bytes 786440 | tf_op jit(solution)/shard_map/ppermute | solution.py:225
  5.6 14.9 %collective-permute-start.17 = (f32[2,128,512]{2,1,0:T(8,128)S(1)}, f32[2,128,512]{2,1,0:T(8,128)S(1)}, u32[]{:S(2)}, u32[]{:S(2)}) collective-permute-start(f32[2,128,512]{2,1,0:T(8,128)S(1)} %collective-permute-done.15.refs_0_.refs_4_), channel_id=1, source_target_pairs={{0,8},{1,9},{2,18},{3,11},{4,12},{5,21},{6,14},{7,15},{8,0},{9,1},... | collective-permute-start | bytes 1572872 | tf_op jit(solution)/shard_map/ppermute | solution.py:233
  20.4 15.2 %collective-permute-start.7 = (f32[1,128,512]{2,1,0:T(8,128)S(1)}, f32[1,128,512]{2,1,0:T(8,128)S(1)}, u32[]{:S(2)}, u32[]{:S(2)}) collective-permute-start(f32[1,128,512]{2,1,0:T(8,128)S(1)} %collective-permute-done.6.refs_4_.refs_2_), channel_id=1, source_target_pairs={{0,8},{8,0},{16,24},{24,16},{1,9},{9,1},{17,25},{25,17},{2,10},{10... | collective-permute-start | bytes 786440 | tf_op jit(solution)/shard_map/ppermute | solution.py:238
  20.5 15.6 %collective-permute-start.10 = (f32[1,128,512]{2,1,0:T(8,128)S(1)}, f32[1,128,512]{2,1,0:T(8,128)S(1)}, u32[]{:S(2)}, u32[]{:S(2)}) collective-permute-start(f32[1,128,512]{2,1,0:T(8,128)S(1)} %collective-permute-done.9.refs_4_), channel_id=1, source_target_pairs={{0,8},{8,0},{16,24},{24,16},{1,9},{9,1},{17,25},{25,17},{2,10},{10... | collective-permute-start | bytes 786440 | tf_op jit(solution)/shard_map/ppermute | solution.py:238
  20.9 32.3 %collective-permute-start.16 = (f32[2,128,512]{2,1,0:T(8,128)S(1)}, f32[2,128,512]{2,1,0:T(8,128)S(1)}, u32[]{:S(2)}, u32[]{:S(2)}) collective-permute-start(f32[2,128,512]{2,1,0:T(8,128)S(1)} %collective-permute-done.15.refs_0_.refs_4_), channel_id=1, source_target_pairs={{0,8},{8,0},{16,24},{24,16},{1,9},{9,1},{17,25},{25,17},{2,10},{10... | collective-permute-start | bytes 1572872 | tf_op jit(solution)/shard_map/ppermute | solution.py:238
  21.0 32.2 %collective-permute-start.18 = (f32[2,128,512]{2,1,0:T(8,128)S(1)}, f32[2,128,512]{2,1,0:T(8,128)S(1)}, u32[]{:S(2)}, u32[]{:S(2)}) collective-permute-start(f32[2,128,512]{2,1,0:T(8,128)S(1)} %collective-permute-done.17.refs_2_.refs_6_), channel_id=1, source_target_pairs={{0,8},{8,0},{16,24},{24,16},{1,9},{9,1},{17,25},{25,17},{2,10},{10... | collective-permute-start | bytes 1572872 | tf_op jit(solution)/shard_map/ppermute | solution.py:238
  22.3 17.1 %collective-permute-start.5 = (f32[128,256]{1,0:T(8,128)S(1)}, f32[128,256]{1,0:T(8,128)S(1)}, u32[]{:S(2)}, u32[]{:S(2)}) collective-permute-start(f32[128,256]{1,0:T(8,128)S(1)} %get-tuple-element.36), channel_id=1, source_target_pairs={{0,1},{1,0},{2,10},{3,4},{4,3},{5,13},{6,7},{7,6},{8,9},{9,8},{10,... | collective-permute-start | bytes 393224 | tf_op jit(solution)/shard_map/ppermute | solution.py:225
  35.6 14.1 %collective-permute-start.22 = (f32[1,128,512]{2,1,0:T(8,128)S(1)}, f32[1,128,512]{2,1,0:T(8,128)S(1)}, u32[]{:S(2)}, u32[]{:S(2)}) collective-permute-start(f32[1,128,512]{2,1,0:T(8,128)S(1)} %collective-permute-done.21.refs_6_), channel_id=1, source_target_pairs={{0,8},{8,0},{16,24},{24,16},{1,9},{9,1},{17,25},{25,17},{2,10},{10... | collective-permute-start | bytes 786440 | tf_op jit(solution)/shard_map/ppermute | solution.py:238
  36.7 6.4 %collective-permute-start.11 = (f32[64,512]{1,0:T(8,128)S(1)}, f32[64,512]{1,0:T(8,128)S(1)}, u32[]{:S(2)}, u32[]{:S(2)}) collective-permute-start(f32[64,512]{1,0:T(8,128)S(1)} %get-tuple-element.40), channel_id=1, source_target_pairs={{0,1},{1,0},{2,10},{3,4},{4,3},{5,13},{6,7},{7,6},{8,9},{9,8},{10,... | collective-permute-start | bytes 393224 | tf_op jit(solution)/shard_map/ppermute | solution.py:225
  39.4 6.1 %collective-permute-start.8 = (f32[128,256]{1,0:T(8,128)S(1)}, f32[128,256]{1,0:T(8,128)S(1)}, u32[]{:S(2)}, u32[]{:S(2)}) collective-permute-start(f32[128,256]{1,0:T(8,128)S(1)} %get-tuple-element.38), channel_id=1, source_target_pairs={{0,1},{1,0},{2,10},{3,4},{4,3},{5,13},{6,7},{7,6},{8,9},{9,8},{10,... | collective-permute-start | bytes 393224 | tf_op jit(solution)/shard_map/ppermute | solution.py:225
  43.2 12.9 %collective-permute-start.14 = (f32[128,512]{1,0:T(8,128)S(1)}, f32[128,512]{1,0:T(8,128)S(1)}, u32[]{:S(2)}, u32[]{:S(2)}) collective-permute-start(f32[128,512]{1,0:T(8,128)S(1)} %get-tuple-element.35.own0), channel_id=1, source_target_pairs={{0,8},{1,9},{3,2},{4,12},{6,5},{7,15},{8,0},{9,1},{11,10},{12,4},{... | collective-permute-start | bytes 786440 | tf_op jit(solution)/shard_map/ppermute | solution.py:225
  45.5 6.8 %collective-permute-start.12 = (f32[64,512]{1,0:T(8,128)S(1)}, f32[64,512]{1,0:T(8,128)S(1)}, u32[]{:S(2)}, u32[]{:S(2)}) collective-permute-start(f32[64,512]{1,0:T(8,128)S(1)} %get-tuple-element.46), channel_id=1, source_target_pairs={{0,1},{1,0},{2,10},{3,4},{4,3},{5,13},{6,7},{7,6},{8,9},{9,8},{10,... | collective-permute-start | bytes 393224 | tf_op jit(solution)/shard_map/ppermute | solution.py:225
  49.7 6.4 %collective-permute-start.13 = (f32[64,512]{1,0:T(8,128)S(1)}, f32[64,512]{1,0:T(8,128)S(1)}, u32[]{:S(2)}, u32[]{:S(2)}) collective-permute-start(f32[64,512]{1,0:T(8,128)S(1)} %get-tuple-element.48), channel_id=1, source_target_pairs={{0,8},{1,2},{2,1},{3,11},{4,5},{5,4},{6,14},{7,15},{8,0},{9,10},{1... | collective-permute-start | bytes 393224 | tf_op jit(solution)/shard_map/ppermute | solution.py:225
  52.3 5.8 %collective-permute-start.23 = (f32[64,512]{1,0:T(8,128)S(1)}, f32[64,512]{1,0:T(8,128)S(1)}, u32[]{:S(2)}, u32[]{:S(2)}) collective-permute-start(f32[64,512]{1,0:T(8,128)S(1)} %get-tuple-element.45.refs_0_), channel_id=1, source_target_pairs={{0,8},{1,9},{2,4},{3,11},{4,2},{5,7},{6,14},{7,5},{8,0},{9,1},{10,... | collective-permute-start | bytes 393224 | tf_op jit(solution)/shard_map/ppermute | solution.py:225
  53.2 5.6 %collective-permute-start.19 = (f32[64,512]{1,0:T(8,128)S(1)}, f32[64,512]{1,0:T(8,128)S(1)}, u32[]{:S(2)}, u32[]{:S(2)}) collective-permute-start(f32[64,512]{1,0:T(8,128)S(1)} %get-tuple-element.54), channel_id=1, source_target_pairs={{0,8},{1,2},{2,1},{3,11},{4,5},{5,4},{6,14},{7,15},{8,0},{9,10},{1... | collective-permute-start | bytes 393224 | tf_op jit(solution)/shard_map/ppermute | solution.py:225
  53.3 6.8 %collective-permute-start.20 = (f32[64,512]{1,0:T(8,128)S(1)}, f32[64,512]{1,0:T(8,128)S(1)}, u32[]{:S(2)}, u32[]{:S(2)}) collective-permute-start(f32[64,512]{1,0:T(8,128)S(1)} %get-tuple-element.47.refs_1_), channel_id=1, source_target_pairs={{0,8},{1,9},{2,4},{3,11},{4,2},{5,7},{6,14},{7,5},{8,0},{9,1},{10,... | collective-permute-start | bytes 393224 | tf_op jit(solution)/shard_map/ppermute | solution.py:225
  58.7 6.3 %collective-permute-start.24 = (f32[64,512]{1,0:T(8,128)S(1)}, f32[64,512]{1,0:T(8,128)S(1)}, u32[]{:S(2)}, u32[]{:S(2)}) collective-permute-start(f32[64,512]{1,0:T(8,128)S(1)} %get-tuple-element.61), channel_id=1, source_target_pairs={{0,8},{1,9},{2,3},{3,2},{4,5},{5,4},{6,14},{7,15},{8,0},{9,1},{10,... | collective-permute-start | bytes 393224 | tf_op jit(solution)/shard_map/ppermute | solution.py:225
  60.6 6.3 %collective-permute-start.25 = (f32[64,512]{1,0:T(8,128)S(1)}, f32[64,512]{1,0:T(8,128)S(1)}, u32[]{:S(2)}, u32[]{:S(2)}) collective-permute-start(f32[64,512]{1,0:T(8,128)S(1)} %get-tuple-element.62), channel_id=1, source_target_pairs={{0,8},{1,9},{2,3},{3,2},{4,12},{5,6},{6,5},{7,15},{8,0},{9,1},{10,... | collective-permute-start | bytes 393224 | tf_op jit(solution)/shard_map/ppermute | solution.py:225
  60.7 11.3 %collective-permute-start.28 = (f32[64,512]{1,0:T(8,128)S(1)}, f32[64,512]{1,0:T(8,128)S(1)}, u32[]{:S(2)}, u32[]{:S(2)}) collective-permute-start(f32[64,512]{1,0:T(8,128)S(1)} %get-tuple-element.64), channel_id=1, source_target_pairs={{0,8},{1,9},{2,4},{3,11},{4,2},{5,7},{6,14},{7,5},{8,0},{9,1},{10,... | collective-permute-start | bytes 393224 | tf_op jit(solution)/shard_map/ppermute | solution.py:225
  65.0 9.1 %collective-permute-start.27 = (f32[64,512]{1,0:T(8,128)S(1)}, f32[64,512]{1,0:T(8,128)S(1)}, u32[]{:S(2)}, u32[]{:S(2)}) collective-permute-start(f32[64,512]{1,0:T(8,128)S(1)} %get-tuple-element.63), channel_id=1, source_target_pairs={{0,8},{1,9},{2,4},{3,11},{4,2},{5,7},{6,14},{7,5},{8,0},{9,1},{10,... | collective-permute-start | bytes 393224 | tf_op jit(solution)/shard_map/ppermute | solution.py:225
  65.0 9.1 %collective-permute-start.26 = (f32[64,512]{1,0:T(8,128)S(1)}, f32[64,512]{1,0:T(8,128)S(1)}, u32[]{:S(2)}, u32[]{:S(2)}) collective-permute-start(f32[64,512]{1,0:T(8,128)S(1)} %collective-permute-done.24.refs_4_), channel_id=1, source_target_pairs={{0,8},{1,9},{2,10},{3,11},{4,6},{5,13},{7,15},{8,0},{9,1},{10,2},{... | collective-permute-start | bytes 393224 | tf_op jit(solution)/shard_map/ppermute | solution.py:225
  (8 other events, 27.6 us)

commit v2 on v1

--- a/solution.py
+++ b/solution.py
@@ -299,8 +299,9 @@
     def ready(numbers, *pieces):
         return call(functools.partial(ready_kernel, ring, numbers), pair(len(numbers)), [], *pieces)
 
-    handed_pairs = ready(((0, 0), (1, 1)), *handed, *handed)
-    last_pairs = ready(((2, 0), (3, 0)), *gathered[2], *mine)
+    handed_pairs = ready(((0, 0), (1, 1), (2, 0)), *handed, *handed, *gathered[2])
+    last_pairs = [*handed_pairs[4:], *ready(((3, 0),), *mine)]
+    handed_pairs = handed_pairs[:4]
     low = block(high=rows // 2)
     buf = pltpu.VMEM((rows // 2, 2 * width), f32)
     own1, onward, fourth = [], [], []

time: 75 us -> 77.8 us (1.037)
  the two profiles are of different devices: /device:TPU:28 before, /device:TPU:24 now
where the time goes in v2:
time: 77.8 us; the launch traced here: 77.6 us
  waiting for transfers between devices  39.1 us (50%)
  starting transfers between devices  30.3 us (39%)
  Pallas kernels  6.5 us (8%)
  local copies, waits for them, and re-layouts  1.42 us (2%)
    ppermute x17, starting transfers between devices, trade(): return lax.ppermute(array, ('row', 'col'), pairs)  25.1 us
    ppermute x5, waiting for transfers between devices, across(): return lax.ppermute(array, ('row', 'col'), pairs)  20.8 us
    ppermute x17, waiting for transfers between devices, trade(): return lax.ppermute(array, ('row', 'col'), pairs)  18.2 us
    pallas_call x11, Pallas kernels, call(): pl.pallas_call(kernel, out_shape=outs, in_specs=[scalars if op.dtype == j...  6.5 us
    ppermute x5, starting transfers between devices, across(): return lax.ppermute(array, ('row', 'col'), pairs)  4.6 us
  transfers between devices with their start and end apart: 29, of which 8 were waited for; matrix products, arithmetic and copies ran while one was open for 2% of the time, Pallas kernels for 7%

profile of v2, /device:TPU:24, one launch (start us, length us, event | category | flops | bytes accessed | tf_op | source)
XLA Modules:
  0.0 77.6 jit_solution(11553916648871780981)
XLA Ops:
  0.0 1.4 %slice_bitcast_fusion = (f32[2,128,512]{2,1,0:T(8,128)S(1)}, f32[2,128,512]{2,1,0:T(8,128)S(1)}) fusion(f32[1,4,128,512]{3,2,1,0:T(8,128)} %param.4), kind=kLoop, calls=%fused_computation | loop fusion | bytes 2097152 | tf_op jit(solution)/shard_map/slice | solution.py:269
  1.4 1.6 %collective-permute-start.3 = (f32[2,128,512]{2,1,0:T(8,128)S(1)}, f32[2,128,512]{2,1,0:T(8,128)S(1)}, u32[]{:S(2)}, u32[]{:S(2)}) collective-permute-start(f32[2,128,512]{2,1,0:T(8,128)S(1)} %get-tuple-element.66), channel_id=1, source_target_pairs={{0,16},{1,17},{2,18},{3,19},{4,20},{5,21},{6,22},{7,23},{8,24},{9,... | collective-permute-start | bytes 1572872 | tf_op jit(solution)/shard_map/ppermute | solution.py:233
  3.0 2.0 %collective-permute-start.15 = (f32[2,128,512]{2,1,0:T(8,128)S(1)}, f32[2,128,512]{2,1,0:T(8,128)S(1)}, u32[]{:S(2)}, u32[]{:S(2)}) collective-permute-start(f32[2,128,512]{2,1,0:T(8,128)S(1)} %get-tuple-element.65), channel_id=1, source_target_pairs={{0,8},{1,2},{3,11},{4,5},{6,14},{7,15},{8,0},{9,10},{11,3},{12,13}... | collective-permute-start | bytes 1572872 | tf_op jit(solution)/shard_map/ppermute | solution.py:225
  5.0 1.6 %collective-permute-start = (f32[128,512]{1,0:T(8,128)S(1)}, f32[128,512]{1,0:T(8,128)S(1)}, u32[]{:S(2)}, u32[]{:S(2)}) collective-permute-start(f32[128,512]{1,0:T(8,128)S(1)} %copy-done.1), channel_id=1, source_target_pairs={{0,1},{1,0},{2,10},{3,4},{4,3},{5,13},{6,7},{7,6},{8,9},{9,8},{10,... | collective-permute-start | bytes 786440 | tf_op jit(solution)/shard_map/ppermute | solution.py:225
  6.7 9.0 %collective-permute-done.3.refs_6_ = f32[2,128,512]{2,1,0:T(8,128)S(1)} collective-permute-done((f32[2,128,512]{2,1,0:T(8,128)S(1)}, f32[2,128,512]{2,1,0:T(8,128)S(1)}, u32[]{:S(2)}, u32[]{:S(2)}) %collective-permute-start.3) | collective-permute-done | bytes 524320 | tf_op jit(solution)/shard_map/ppermute | solution.py:233
  16.2 1.5 %collective-permute-start.6 = (f32[1,128,512]{2,1,0:T(8,128)S(1)}, f32[1,128,512]{2,1,0:T(8,128)S(1)}, u32[]{:S(2)}, u32[]{:S(2)}) collective-permute-start(f32[1,128,512]{2,1,0:T(8,128)S(1)} %get-tuple-element.68), channel_id=1, source_target_pairs={{0,16},{1,9},{2,18},{3,19},{4,12},{5,21},{6,22},{7,15},{8,24},{9,1... | collective-permute-start | bytes 786440 | tf_op jit(solution)/shard_map/ppermute | solution.py:233
  18.2 7.1 %collective-permute-done.6.refs_4_.refs_10_ = f32[1,128,512]{2,1,0:T(8,128)S(1)} collective-permute-done((f32[1,128,512]{2,1,0:T(8,128)S(1)}, f32[1,128,512]{2,1,0:T(8,128)S(1)}, u32[]{:S(2)}, u32[]{:S(2)}) %collective-permute-start.6) | collective-permute-done | bytes 262176 | tf_op jit(solution)/shard_map/ppermute | solution.py:233
  25.4 4.7 %collective-permute-done.9.refs_4_ = f32[1,128,512]{2,1,0:T(8,128)S(1)} collective-permute-done((f32[1,128,512]{2,1,0:T(8,128)S(1)}, f32[1,128,512]{2,1,0:T(8,128)S(1)}, u32[]{:S(2)}, u32[]{:S(2)}) %collective-permute-start.9) | collective-permute-done | bytes 262176 | tf_op jit(solution)/shard_map/ppermute | solution.py:233
  31.2 1.7 %shard_map.37 = (f32[128,512]{1,0:T(8,128)S(1)}, f32[128,1024]{1,0:T(8,128)S(1)}, f32[128,256]{1,0:T(8,128)S(1)}, bf16[512,512]{1,0:T(8,128)(2,1)S(1)}, bf16[512...) custom-call(s32[8]{0:T(128)S(1)} %copy-done.2, f32[128,512]{1,0:T(8,128)S(1)} %copy-done.1, ...), custom_call_target="tpu_custom_call" | custom-call | tf_op jit(solution)/shard_map/pallas_call | solution.py:244
  32.9 0.6 shard_map.38
  33.6 0.6 shard_map.39
  34.4 1.9 %collective-permute-start.8 = (f32[128,256]{1,0:T(8,128)S(1)}, f32[128,256]{1,0:T(8,128)S(1)}, u32[]{:S(2)}, u32[]{:S(2)}) collective-permute-start(f32[128,256]{1,0:T(8,128)S(1)} %get-tuple-element.38), channel_id=1, source_target_pairs={{0,1},{1,0},{2,10},{3,4},{4,3},{5,13},{6,7},{7,6},{8,9},{9,8},{10,... | collective-permute-start | bytes 393224 | tf_op jit(solution)/shard_map/ppermute | solution.py:225
  36.3 4.3 %collective-permute-done.11.refs_3_ = f32[64,512]{1,0:T(8,128)S(1)} collective-permute-done((f32[64,512]{1,0:T(8,128)S(1)}, f32[64,512]{1,0:T(8,128)S(1)}, u32[]{:S(2)}, u32[]{:S(2)}) %collective-permute-start.11) | collective-permute-done | bytes 131104 | tf_op jit(solution)/shard_map/ppermute | solution.py:225
  40.6 2.8 %collective-permute-done.8.refs_2_ = f32[128,256]{1,0:T(8,128)S(1)} collective-permute-done((f32[128,256]{1,0:T(8,128)S(1)}, f32[128,256]{1,0:T(8,128)S(1)}, u32[]{:S(2)}, u32[]{:S(2)}) %collective-permute-start.8) | collective-permute-done | bytes 131104 | tf_op jit(solution)/shard_map/ppermute | solution.py:225
  43.4 7.9 %collective-permute-start.14 = (f32[128,512]{1,0:T(8,128)S(1)}, f32[128,512]{1,0:T(8,128)S(1)}, u32[]{:S(2)}, u32[]{:S(2)}) collective-permute-start(f32[128,512]{1,0:T(8,128)S(1)} %get-tuple-element.35.own0), channel_id=1, source_target_pairs={{0,8},{1,9},{3,2},{4,12},{6,5},{7,15},{8,0},{9,1},{11,10},{12,4},{... | collective-permute-start | bytes 786440 | tf_op jit(solution)/shard_map/ppermute | solution.py:225
  51.4 0.6 shard_map.40
  52.1 4.6 %collective-permute-done.12.refs_3_ = f32[64,512]{1,0:T(8,128)S(1)} collective-permute-done((f32[64,512]{1,0:T(8,128)S(1)}, f32[64,512]{1,0:T(8,128)S(1)}, u32[]{:S(2)}, u32[]{:S(2)}) %collective-permute-start.12) | collective-permute-done | bytes 131104 | tf_op jit(solution)/shard_map/ppermute | solution.py:225
  57.3 0.6 collective-permute-start.19
  58.5 0.6 shard_map.46
  60.2 8.8 %collective-permute-start.25 = (f32[64,512]{1,0:T(8,128)S(1)}, f32[64,512]{1,0:T(8,128)S(1)}, u32[]{:S(2)}, u32[]{:S(2)}) collective-permute-start(f32[64,512]{1,0:T(8,128)S(1)} %get-tuple-element.62), channel_id=1, source_target_pairs={{0,8},{1,9},{2,3},{3,2},{4,12},{5,6},{6,5},{7,15},{8,0},{9,1},{10,... | collective-permute-start | bytes 393224 | tf_op jit(solution)/shard_map/ppermute | solution.py:225
  69.0 1.3 %collective-permute-start.26 = (f32[64,512]{1,0:T(8,128)S(1)}, f32[64,512]{1,0:T(8,128)S(1)}, u32[]{:S(2)}, u32[]{:S(2)}) collective-permute-start(f32[64,512]{1,0:T(8,128)S(1)} %collective-permute-done.24.refs_4_), channel_id=1, source_target_pairs={{0,8},{1,9},{2,10},{3,11},{4,6},{5,13},{7,15},{8,0},{9,1},{10,2},{... | collective-permute-start | bytes 393224 | tf_op jit(solution)/shard_map/ppermute | solution.py:225
  70.3 3.0 %collective-permute-done.25.refs_5_.refs_7_ = f32[64,512]{1,0:T(8,128)S(1)} collective-permute-done((f32[64,512]{1,0:T(8,128)S(1)}, f32[64,512]{1,0:T(8,128)S(1)}, u32[]{:S(2)}, u32[]{:S(2)}) %collective-permute-start.25) | collective-permute-done | bytes 131104 | tf_op jit(solution)/shard_map/ppermute | solution.py:225
  73.4 3.4 %collective-permute-done.26.refs_6_ = f32[64,512]{1,0:T(8,128)S(1)} collective-permute-done((f32[64,512]{1,0:T(8,128)S(1)}, f32[64,512]{1,0:T(8,128)S(1)}, u32[]{:S(2)}, u32[]{:S(2)}) %collective-permute-start.26) | collective-permute-done | bytes 131104 | tf_op jit(solution)/shard_map/ppermute | solution.py:225
  76.8 0.7 shard_map.47
  (53 shorter events, 5.0 us)
Async XLA Ops:
  0.0 30.1 %collective-permute-start.2 = (f32[4,128,512]{2,1,0:T(8,128)}, f32[4,128,512]{2,1,0:T(8,128)S(1)}, u32[]{:S(2)}, u32[]{:S(2)}) collective-permute-start(f32[4,128,512]{2,1,0:T(8,128)} %bitcast.9), channel_id=1, source_target_pairs={{0,8},{8,0},{16,24},{24,16},{1,9},{9,1},{17,25},{25,17},{2,10},{10... | collective-permute-start | bytes 3145736 | tf_op jit(solution)/shard_map/ppermute | solution.py:238
  1.4 14.3 %collective-permute-start.3 = (f32[2,128,512]{2,1,0:T(8,128)S(1)}, f32[2,128,512]{2,1,0:T(8,128)S(1)}, u32[]{:S(2)}, u32[]{:S(2)}) collective-permute-start(f32[2,128,512]{2,1,0:T(8,128)S(1)} %get-tuple-element.66), channel_id=1, source_target_pairs={{0,16},{1,17},{2,18},{3,19},{4,20},{5,21},{6,22},{7,23},{8,24},{9,... | collective-permute-start | bytes 1572872 | tf_op jit(solution)/shard_map/ppermute | solution.py:233
  3.0 12.7 %collective-permute-start.15 = (f32[2,128,512]{2,1,0:T(8,128)S(1)}, f32[2,128,512]{2,1,0:T(8,128)S(1)}, u32[]{:S(2)}, u32[]{:S(2)}) collective-permute-start(f32[2,128,512]{2,1,0:T(8,128)S(1)} %get-tuple-element.65), channel_id=1, source_target_pairs={{0,8},{1,2},{3,11},{4,5},{6,14},{7,15},{8,0},{9,10},{11,3},{12,13}... | collective-permute-start | bytes 1572872 | tf_op jit(solution)/shard_map/ppermute | solution.py:225
  5.0 11.2 %collective-permute-start = (f32[128,512]{1,0:T(8,128)S(1)}, f32[128,512]{1,0:T(8,128)S(1)}, u32[]{:S(2)}, u32[]{:S(2)}) collective-permute-start(f32[128,512]{1,0:T(8,128)S(1)} %copy-done.1), channel_id=1, source_target_pairs={{0,1},{1,0},{2,10},{3,4},{4,3},{5,13},{6,7},{7,6},{8,9},{9,8},{10,... | collective-permute-start | bytes 786440 | tf_op jit(solution)/shard_map/ppermute | solution.py:225
  6.6 11.1 %collective-permute-start.1 = (f32[128,512]{1,0:T(8,128)S(1)}, f32[128,512]{1,0:T(8,128)S(1)}, u32[]{:S(2)}, u32[]{:S(2)}) collective-permute-start(f32[128,512]{1,0:T(8,128)S(1)} %copy-done.1), channel_id=1, source_target_pairs={{0,2},{1,9},{2,0},{3,5},{4,12},{5,3},{6,14},{7,15},{8,10},{9,1},{1... | collective-permute-start | bytes 786440 | tf_op jit(solution)/shard_map/ppermute | solution.py:225
  15.7 14.9 %collective-permute-start.4 = (f32[2,128,512]{2,1,0:T(8,128)S(1)}, f32[2,128,512]{2,1,0:T(8,128)S(1)}, u32[]{:S(2)}, u32[]{:S(2)}) collective-permute-start(f32[2,128,512]{2,1,0:T(8,128)S(1)} %collective-permute-done.3.refs_6_), channel_id=1, source_target_pairs={{0,8},{8,0},{16,24},{24,16},{1,9},{9,1},{17,25},{25,17},{2,10},{10... | collective-permute-start | bytes 1572872 | tf_op jit(solution)/shard_map/ppermute | solution.py:238
  15.7 15.0 %collective-permute-start.17 = (f32[2,128,512]{2,1,0:T(8,128)S(1)}, f32[2,128,512]{2,1,0:T(8,128)S(1)}, u32[]{:S(2)}, u32[]{:S(2)}) collective-permute-start(f32[2,128,512]{2,1,0:T(8,128)S(1)} %collective-permute-done.15.refs_0_.refs_4_), channel_id=1, source_target_pairs={{0,8},{1,9},{2,18},{3,11},{4,12},{5,21},{6,14},{7,15},{8,0},{9,1},... | collective-permute-start | bytes 1572872 | tf_op jit(solution)/shard_map/ppermute | solution.py:233
  16.2 9.2 %collective-permute-start.6 = (f32[1,128,512]{2,1,0:T(8,128)S(1)}, f32[1,128,512]{2,1,0:T(8,128)S(1)}, u32[]{:S(2)}, u32[]{:S(2)}) collective-permute-start(f32[1,128,512]{2,1,0:T(8,128)S(1)} %get-tuple-element.68), channel_id=1, source_target_pairs={{0,16},{1,9},{2,18},{3,19},{4,12},{5,21},{6,22},{7,15},{8,24},{9,1... | collective-permute-start | bytes 786440 | tf_op jit(solution)/shard_map/ppermute | solution.py:233
  17.7 12.4 %collective-permute-start.9 = (f32[1,128,512]{2,1,0:T(8,128)S(1)}, f32[1,128,512]{2,1,0:T(8,128)S(1)}, u32[]{:S(2)}, u32[]{:S(2)}) collective-permute-start(f32[1,128,512]{2,1,0:T(8,128)S(1)} %get-tuple-element.67), channel_id=1, source_target_pairs={{0,16},{1,9},{2,10},{3,19},{4,12},{5,13},{6,22},{7,15},{8,24},{9,1... | collective-permute-start | bytes 786440 | tf_op jit(solution)/shard_map/ppermute | solution.py:233
  25.4 7.5 %collective-permute-start.7 = (f32[1,128,512]{2,1,0:T(8,128)S(1)}, f32[1,128,512]{2,1,0:T(8,128)S(1)}, u32[]{:S(2)}, u32[]{:S(2)}) collective-permute-start(f32[1,128,512]{2,1,0:T(8,128)S(1)} %collective-permute-done.6.refs_4_.refs_10_), channel_id=1, source_target_pairs={{0,8},{8,0},{16,24},{24,16},{1,9},{9,1},{17,25},{25,17},{2,10},{10... | collective-permute-start | bytes 786440 | tf_op jit(solution)/shard_map/ppermute | solution.py:238
  30.6 26.6 %collective-permute-start.16 = (f32[2,128,512]{2,1,0:T(8,128)S(1)}, f32[2,128,512]{2,1,0:T(8,128)S(1)}, u32[]{:S(2)}, u32[]{:S(2)}) collective-permute-start(f32[2,128,512]{2,1,0:T(8,128)S(1)} %collective-permute-done.15.refs_0_.refs_4_), channel_id=1, source_target_pairs={{0,8},{8,0},{16,24},{24,16},{1,9},{9,1},{17,25},{25,17},{2,10},{10... | collective-permute-start | bytes 1572872 | tf_op jit(solution)/shard_map/ppermute | solution.py:238
  30.7 27.1 %collective-permute-start.18 = (f32[2,128,512]{2,1,0:T(8,128)S(1)}, f32[2,128,512]{2,1,0:T(8,128)S(1)}, u32[]{:S(2)}, u32[]{:S(2)}) collective-permute-start(f32[2,128,512]{2,1,0:T(8,128)S(1)} %collective-permute-done.17.refs_2_.refs_6_), channel_id=1, source_target_pairs={{0,8},{8,0},{16,24},{24,16},{1,9},{9,1},{17,25},{25,17},{2,10},{10... | collective-permute-start | bytes 1572872 | tf_op jit(solution)/shard_map/ppermute | solution.py:238
  34.2 6.4 %collective-permute-start.11 = (f32[64,512]{1,0:T(8,128)S(1)}, f32[64,512]{1,0:T(8,128)S(1)}, u32[]{:S(2)}, u32[]{:S(2)}) collective-permute-start(f32[64,512]{1,0:T(8,128)S(1)} %get-tuple-element.40), channel_id=1, source_target_pairs={{0,1},{1,0},{2,10},{3,4},{4,3},{5,13},{6,7},{7,6},{8,9},{9,8},{10,... | collective-permute-start | bytes 393224 | tf_op jit(solution)/shard_map/ppermute | solution.py:225
  34.3 17.7 %collective-permute-start.22 = (f32[1,128,512]{2,1,0:T(8,128)S(1)}, f32[1,128,512]{2,1,0:T(8,128)S(1)}, u32[]{:S(2)}, u32[]{:S(2)}) collective-permute-start(f32[1,128,512]{2,1,0:T(8,128)S(1)} %collective-permute-done.21.refs_2_), channel_id=1, source_target_pairs={{0,8},{8,0},{16,24},{24,16},{1,9},{9,1},{17,25},{25,17},{2,10},{10... | collective-permute-start | bytes 786440 | tf_op jit(solution)/shard_map/ppermute | solution.py:238
  34.4 9.0 %collective-permute-start.8 = (f32[128,256]{1,0:T(8,128)S(1)}, f32[128,256]{1,0:T(8,128)S(1)}, u32[]{:S(2)}, u32[]{:S(2)}) collective-permute-start(f32[128,256]{1,0:T(8,128)S(1)} %get-tuple-element.38), channel_id=1, source_target_pairs={{0,1},{1,0},{2,10},{3,4},{4,3},{5,13},{6,7},{7,6},{8,9},{9,8},{10,... | collective-permute-start | bytes 393224 | tf_op jit(solution)/shard_map/ppermute | solution.py:225
  40.6 10.7 %collective-permute-start.5 = (f32[128,256]{1,0:T(8,128)S(1)}, f32[128,256]{1,0:T(8,128)S(1)}, u32[]{:S(2)}, u32[]{:S(2)}) collective-permute-start(f32[128,256]{1,0:T(8,128)S(1)} %get-tuple-element.36), channel_id=1, source_target_pairs={{0,1},{1,0},{2,10},{3,4},{4,3},{5,13},{6,7},{7,6},{8,9},{9,8},{10,... | collective-permute-start | bytes 393224 | tf_op jit(solution)/shard_map/ppermute | solution.py:225
  43.4 14.5 %collective-permute-start.14 = (f32[128,512]{1,0:T(8,128)S(1)}, f32[128,512]{1,0:T(8,128)S(1)}, u32[]{:S(2)}, u32[]{:S(2)}) collective-permute-start(f32[128,512]{1,0:T(8,128)S(1)} %get-tuple-element.35.own0), channel_id=1, source_target_pairs={{0,8},{1,9},{3,2},{4,12},{6,5},{7,15},{8,0},{9,1},{11,10},{12,4},{... | collective-permute-start | bytes 786440 | tf_op jit(solution)/shard_map/ppermute | solution.py:225
  51.3 5.3 %collective-permute-start.12 = (f32[64,512]{1,0:T(8,128)S(1)}, f32[64,512]{1,0:T(8,128)S(1)}, u32[]{:S(2)}, u32[]{:S(2)}) collective-permute-start(f32[64,512]{1,0:T(8,128)S(1)} %get-tuple-element.46), channel_id=1, source_target_pairs={{0,1},{1,0},{2,10},{3,4},{4,3},{5,13},{6,7},{7,6},{8,9},{9,8},{10,... | collective-permute-start | bytes 393224 | tf_op jit(solution)/shard_map/ppermute | solution.py:225
  52.0 5.9 %collective-permute-start.13 = (f32[64,512]{1,0:T(8,128)S(1)}, f32[64,512]{1,0:T(8,128)S(1)}, u32[]{:S(2)}, u32[]{:S(2)}) collective-permute-start(f32[64,512]{1,0:T(8,128)S(1)} %get-tuple-element.48), channel_id=1, source_target_pairs={{0,8},{1,2},{2,1},{3,11},{4,5},{5,4},{6,14},{7,15},{8,0},{9,10},{1... | collective-permute-start | bytes 393224 | tf_op jit(solution)/shard_map/ppermute | solution.py:225
  59.1 10.0 %collective-permute-start.24 = (f32[64,512]{1,0:T(8,128)S(1)}, f32[64,512]{1,0:T(8,128)S(1)}, u32[]{:S(2)}, u32[]{:S(2)}) collective-permute-start(f32[64,512]{1,0:T(8,128)S(1)} %get-tuple-element.61), channel_id=1, source_target_pairs={{0,8},{1,9},{2,3},{3,2},{4,5},{5,4},{6,14},{7,15},{8,0},{9,1},{10,... | collective-permute-start | bytes 393224 | tf_op jit(solution)/shard_map/ppermute | solution.py:225
  59.6 10.8 %collective-permute-start.27 = (f32[64,512]{1,0:T(8,128)S(1)}, f32[64,512]{1,0:T(8,128)S(1)}, u32[]{:S(2)}, u32[]{:S(2)}) collective-permute-start(f32[64,512]{1,0:T(8,128)S(1)} %get-tuple-element.63), channel_id=1, source_target_pairs={{0,8},{1,9},{2,4},{3,11},{4,2},{5,7},{6,14},{7,5},{8,0},{9,1},{10,... | collective-permute-start | bytes 393224 | tf_op jit(solution)/shard_map/ppermute | solution.py:225
  60.2 13.2 %collective-permute-start.25 = (f32[64,512]{1,0:T(8,128)S(1)}, f32[64,512]{1,0:T(8,128)S(1)}, u32[]{:S(2)}, u32[]{:S(2)}) collective-permute-start(f32[64,512]{1,0:T(8,128)S(1)} %get-tuple-element.62), channel_id=1, source_target_pairs={{0,8},{1,9},{2,3},{3,2},{4,12},{5,6},{6,5},{7,15},{8,0},{9,1},{10,... | collective-permute-start | bytes 393224 | tf_op jit(solution)/shard_map/ppermute | solution.py:225
  69.0 4.4 %collective-permute-start.28 = (f32[64,512]{1,0:T(8,128)S(1)}, f32[64,512]{1,0:T(8,128)S(1)}, u32[]{:S(2)}, u32[]{:S(2)}) collective-permute-start(f32[64,512]{1,0:T(8,128)S(1)} %get-tuple-element.64), channel_id=1, source_target_pairs={{0,8},{1,9},{2,4},{3,11},{4,2},{5,7},{6,14},{7,5},{8,0},{9,1},{10,... | collective-permute-start | bytes 393224 | tf_op jit(solution)/shard_map/ppermute | solution.py:225
  69.0 7.8 %collective-permute-start.26 = (f32[64,512]{1,0:T(8,128)S(1)}, f32[64,512]{1,0:T(8,128)S(1)}, u32[]{:S(2)}, u32[]{:S(2)}) collective-permute-start(f32[64,512]{1,0:T(8,128)S(1)} %collective-permute-done.24.refs_4_), channel_id=1, source_target_pairs={{0,8},{1,9},{2,10},{3,11},{4,6},{5,13},{7,15},{8,0},{9,1},{10,2},{... | collective-permute-start | bytes 393224 | tf_op jit(solution)/shard_map/ppermute | solution.py:225
  (8 other events, 40.2 us)
